TPU v7x, 32 devices: a whole 2x2x4 slice. The times are simulated.
32 devices in a mesh: section: 8 (over y, x, core), fsdp: 4 (over z).
Axes of the slice: x: 2, y: 2, z: 4, core: 2. Of those that a mesh axis runs over, the one named last changes fastest.
Arguments:
- layer_input: bfloat16 [8, 512, 4096], P('section', 'fsdp'), may hold values from -6 to 6
- next_cot: bfloat16 [8, 512, 512], P('section', 'fsdp'), may hold values from -6 to 6
- w_value: bfloat16 [8, 4096, 512], P('section', 'fsdp'), may hold values from -0.25 to 0.25
- micro_ids: int32 [8, 4], P('section', 'fsdp'), may hold values from 0 to 1
Outputs:
- grad_input: bfloat16 [8, 512, 4096], P('section', 'fsdp')
- grad_sum: float32 [8, 4096, 512], P('section', 'fsdp')
- grad_square: float32 [8, 4096, 512], P('section', 'fsdp')
All inputs are finite; a program needn't handle non-finite values.
Results may differ from a plain program's by a relative error of at most 0.0037.
Values may be sent and summed in bfloat16 or wider, within the bound.
A program may use at most 64 MiB of HBM per device.

v0:
```python
import jax
import jax.numpy as jnp
from jax import lax
from jax.sharding import PartitionSpec as P

MICRO = 2


def from_behind(value, axis, steps):
    count = lax.axis_size(axis)
    pairs = [(source, (source + steps) % count) for source in range(count)]
    return lax.ppermute(value, axis, pairs)


def body(layer_input, next_cot, w_value, micro_ids):
    inputs_local = layer_input[0]
    incoming = from_behind(next_cot, "section", -1)[0]
    weight_local = w_value[0]
    fsdp_count = lax.axis_size("fsdp")
    token_count = inputs_local.shape[0]
    row_share = weight_local.shape[0]
    columns = weight_local.shape[1]
    inverse = 1.0 / token_count
    owned = lax.all_to_all(inputs_local, "fsdp", split_axis=1, concat_axis=0, tiled=True)
    cot_all, micro_all = (
        lax.all_gather(incoming, "fsdp", axis=0, tiled=True),
        lax.all_gather(micro_ids, "fsdp", axis=1, tiled=True),
    )
    owner_cols = lax.dot_general(
        cot_all, weight_local, (((1,), (1,)), ((), ())), preferred_element_type=jnp.float32
    ).astype(jnp.bfloat16)
    grad_input = lax.all_to_all(owner_cols, "fsdp", split_axis=0, concat_axis=1, tiled=True)
    owned = owned.reshape(fsdp_count, token_count, row_share)
    cot_blocks = cot_all.reshape(fsdp_count, token_count, columns)
    partial_value = (
        jnp.einsum("ftd,ftc->fdc", owned, cot_blocks, preferred_element_type=jnp.float32) * inverse
    )
    partial_value = lax.optimization_barrier(partial_value.astype(jnp.bfloat16)).astype(jnp.float32)
    onehot = (micro_all[0][:, None] == jnp.arange(MICRO, dtype=jnp.int32)[None, :]).astype(
        jnp.float32
    )
    stacked = jnp.einsum("fm,fdc->mdc", onehot, partial_value)
    grad_sum = jnp.sum(stacked, axis=0)
    grad_square = jnp.sum(stacked * stacked, axis=0)
    return (grad_input[None], grad_sum[None], grad_square[None])


def solution(mesh):
    return jax.shard_map(
        body,
        mesh=mesh,
        in_specs=(
            P("section", "fsdp", None),
            P("section", "fsdp", None),
            P("section", "fsdp", None),
            P("section", "fsdp"),
        ),
        out_specs=(
            P("section", "fsdp", None),
            P("section", "fsdp", None),
            P("section", "fsdp", None),
        ),
        check_vma=False,
    )
```

profile of v0, /device:TPU:0, one launch (start us, length us, event | category | flops | bytes accessed | tf_op | source)
XLA Modules:
  0.0 94.9 jit_solution(13938566455108437013)
XLA Ops:
  0.6 0.0 copy-start
  0.6 0.0 copy-start.2
  0.7 1.7 %copy.10 = bf16[1,128,4096]{1,2,0:T(8,128)(2,1)S(1)} copy(bf16[1,128,4096]{2,1,0:T(8,128)(2,1)} %param.4) | data formatting | bytes 2097152 | tf_op args[0]
  2.4 1.3 %copy.11 = bf16[128,4,1024]{2,0,1:T(8,128)(2,1)} copy(bf16[128,4,1024]{0,2,1:T(8,128)(2,1)S(1)} %bitcast.25) | data formatting | bytes 2097152 | tf_op jit(solution)/shard_map/all_to_all | solution.py:24
  3.7 0.0 copy-start.3
  3.7 6.5 %all-to-all-start.1 = ((bf16[128,4,1024]{2,0,1:T(8,128)(2,1)}), bf16[128,4,1024]{2,0,1:T(8,128)(2,1)S(1)}, u32[]{:S(2)}, u32[]{:S(2)}) async-start(bf16[128,4,1024]{2,0,1:T(8,128)(2,1)} %copy.11), calls=%async_computation.1 | async-start | bytes 2097152 | tf_op jit(solution)/shard_map/all_to_all | solution.py:24
  10.2 0.0 copy-done.2
  10.2 1.6 %collective-permute-start = (bf16[1,128,512]{2,1,0:T(8,128)(2,1)S(1)}, bf16[1,128,512]{2,1,0:T(8,128)(2,1)S(1)}, u32[]{:S(2)}, u32[]{:S(2)}) collective-permute-start(bf16[1,128,512]{2,1,0:T(8,128)(2,1)S(1)} %copy-done.2), channel_id=1, source_target_pairs={{0,28},{4,0},{8,4},{12,8},{16,12},{20,16},{24,20},{28,24},{1,29},{... | collective-permute-start | bytes 393224 | tf_op jit(solution)/shard_map/ppermute | solution.py:12
  11.8 2.5 %collective-permute-done = bf16[1,128,512]{2,1,0:T(8,128)(2,1)S(1)} collective-permute-done((bf16[1,128,512]{2,1,0:T(8,128)(2,1)S(1)}, bf16[1,128,512]{2,1,0:T(8,128)(2,1)S(1)}, u32[]{:S(2)}, u32[]{:S(2)}) %collective-permute-start) | collective-permute-done | bytes 131104 | tf_op jit(solution)/shard_map/ppermute | solution.py:12
  14.3 32.0 %all-gather = bf16[1,512,512]{2,1,0:T(8,128)(2,1)S(1)} all-gather(bf16[1,128,512]{2,1,0:T(8,128)(2,1)S(1)} %collective-permute-done), channel_id=2, replica_groups=mesh['section'=8,'fsdp'=4] {'fsdp'}, dimensions={1}, use_global_device_ids=true | all-gather | bytes 655360 | tf_op jit(solution)/shard_map/all_gather | solution.py:26
  46.3 0.0 copy-start.1
  46.3 0.8 copy-done.1
  47.1 0.0 copy-done
  47.1 1.7 %convolution_convert_fusion = bf16[512,1024]{1,0:T(8,128)(2,1)} fusion(bf16[1,1024,512]{2,1,0:T(8,128)(2,1)S(1)} %copy-done, bf16[1,512,512]{2,1,0:T(8,128)(2,1)S(1)} %all-gather), kind=kOutput, calls=%fused_computation.4 | convolution fusion | flops 537395200 | bytes 2621440 | tf_op jit(solution)/shard_map/dot_general | solution.py:29
  48.8 0.0 all-to-all-done.1
  48.8 4.6 %all-to-all-start = ((bf16[4,128,1024]{2,1,0:T(8,128)(2,1)}), bf16[4,128,1024]{2,1,0:T(8,128)(2,1)S(1)}, u32[]{:S(2)}, u32[]{:S(2)}) async-start(bf16[4,128,1024]{2,1,0:T(8,128)(2,1)} %bitcast.27), calls=%async_computation | async-start | bytes 2097152 | tf_op jit(solution)/shard_map/all_to_all | solution.py:32
  54.1 0.0 copy-done.3
  54.1 0.6 dynamic-slice
  54.7 0.7 bitcast_dynamic-update-slice_fusion
  55.3 20.2 %all-reduce = s32[4]{0:T(128)S(1)} all-reduce(s32[4]{0:T(128)S(1)} %bitcast_dynamic-update-slice_fusion), channel_id=1, replica_groups=mesh['section'=8,'fsdp'=4] {'fsdp'}, use_global_device_ids=true, to_apply=%add | all-reduce | flops 4 | bytes 32
  75.6 1.3 %copy.12 = bf16[128,4,1024]{0,2,1:T(8,128)(2,1)} copy(bf16[128,4,1024]{2,0,1:T(8,128)(2,1)S(1)} %all-to-all-done.1) | data formatting | bytes 2097152 | tf_op jit(solution)/shard_map/all_to_all | solution.py:24
  76.9 2.6 %multiply_convert_fusion = bf16[4,1024,512]{2,1,0:T(8,128)(2,1)S(1)} fusion(bf16[4,128,512]{2,1,0:T(8,128)(2,1)} %bitcast.26, bf16[128,4,1024]{0,2,1:T(8,128)(2,1)} %copy.12), kind=kOutput, calls=%fused_computation | convolution fusion | flops 541065216 | bytes 5767168 | tf_op jit(solution)/shard_map/ftd,ftc->fdc/dot_general | solution.py:36
  79.4 13.0 %multiply_reduce_fusion = (f32[1024,512]{1,0:T(8,128)}, f32[1024,512]{1,0:T(8,128)}) fusion(bf16[4,1024,512]{2,1,0:T(8,128)(2,1)S(1)} %multiply_convert_fusion, s32[4]{0:T(128)S(1)} %all-reduce), kind=kOutput, calls=%fused_computation.1 | convolution fusion | flops 10485768 | bytes 8388624 | tf_op jit(solution)/shard_map/fm,fdc->mdc/dot_general | solution.py:42
  92.5 0.0 all-to-all-done
  92.5 0.8 copy.9
  93.3 1.6 %broadcast_in_dim.10 = bf16[1,128,4096]{2,1,0:T(8,128)(2,1)} reshape(bf16[128,4,1024]{2,1,0:T(4,128)(2,1)S(1)} %copy.9) | data formatting | bytes 2097152 | tf_op jit(solution)/shard_map/broadcast_in_dim | solution.py:45
  (1 shorter events, 0.0 us)
Async XLA Ops:
  0.6 46.5 %copy-start = (bf16[1,1024,512]{2,1,0:T(8,128)(2,1)S(1)}, bf16[1,1024,512]{2,1,0:T(8,128)(2,1)}, u32[]{:S(2)}) copy-start(bf16[1,1024,512]{2,1,0:T(8,128)(2,1)} %param.6) | copy-start | bytes 3145732
  0.6 9.5 %copy-start.2 = (bf16[1,128,512]{2,1,0:T(8,128)(2,1)S(1)}, bf16[1,128,512]{2,1,0:T(8,128)(2,1)}, u32[]{:S(2)}) copy-start(bf16[1,128,512]{2,1,0:T(8,128)(2,1)} %param.5) | copy-start | bytes 393220
  3.7 50.4 %copy-start.3 = (u32[32]{0:T(128)S(1)}, u32[32]{0:T(128)}, u32[]{:S(2)}) copy-start(u32[32]{0:T(128)} %constant.10) | copy-start | bytes 388
  3.7 45.1 %all-to-all-start.1 = ((bf16[128,4,1024]{2,0,1:T(8,128)(2,1)}), bf16[128,4,1024]{2,0,1:T(8,128)(2,1)S(1)}, u32[]{:S(2)}, u32[]{:S(2)}) async-start(bf16[128,4,1024]{2,0,1:T(8,128)(2,1)} %copy.11), calls=%async_computation.1 | async-start | bytes 2097152 | tf_op jit(solution)/shard_map/all_to_all | solution.py:24
  10.2 4.1 %collective-permute-start = (bf16[1,128,512]{2,1,0:T(8,128)(2,1)S(1)}, bf16[1,128,512]{2,1,0:T(8,128)(2,1)S(1)}, u32[]{:S(2)}, u32[]{:S(2)}) collective-permute-start(bf16[1,128,512]{2,1,0:T(8,128)(2,1)S(1)} %copy-done.2), channel_id=1, source_target_pairs={{0,28},{4,0},{8,4},{12,8},{16,12},{20,16},{24,20},{28,24},{1,29},{... | collective-permute-start | bytes 393224 | tf_op jit(solution)/shard_map/ppermute | solution.py:12
  46.3 0.8 copy-start.1
  48.8 43.7 %all-to-all-start = ((bf16[4,128,1024]{2,1,0:T(8,128)(2,1)}), bf16[4,128,1024]{2,1,0:T(8,128)(2,1)S(1)}, u32[]{:S(2)}, u32[]{:S(2)}) async-start(bf16[4,128,1024]{2,1,0:T(8,128)(2,1)} %bitcast.27), calls=%async_computation | async-start | bytes 2097152 | tf_op jit(solution)/shard_map/all_to_all | solution.py:32
where the time goes:
time: 95.2 us; the launch traced here: 94.9 us
  blocking collectives  52.2 us (55%)
  matrix products  17.4 us (18%)
  starting transfers between devices  12.7 us (13%)
  local copies, waits for them, and re-layouts  8.82 us (9%)
  waiting for transfers between devices  2.53 us (3%)
  between operations  1.34 us (1%)
    all_gather x1, blocking collectives, body(): lax.all_gather(incoming, 'fsdp', axis=0, tiled=True)  32 us
    unnamed x1, blocking collectives  20.2 us
    dot_general x1, matrix products, body(): stacked = jnp.einsum('fm,fdc->mdc', onehot, partial_value)  13 us
    all_to_all x1, starting transfers between devices, body(): lax.all_to_all(inputs_local, 'fsdp', split_axis=1, concat_axis=0, tiled=T...  6.48 us
    all_to_all x1, starting transfers between devices, body(): lax.all_to_all(owner_cols, 'fsdp', split_axis=0, concat_axis=1, tiled=True)  4.58 us
    unnamed x12, local copies, waits for them, and re-layouts  3.8 us
    all_to_all x2, local copies, waits for them, and re-layouts, body(): lax.all_to_all(inputs_local, 'fsdp', split_axis=1, concat_axis=0, tiled=T...  2.61 us
    dot_general x1, matrix products, body(): jnp.einsum('ftd,ftc->fdc', owned, cot_blocks, preferred_element_type=jnp....  2.59 us
  transfers between devices with their start and end apart: 3, of which 1 were waited for; matrix products, arithmetic and copies ran while one was open for 21% of the time, Pallas kernels for 0%

commit v1 on v0

--- a/solution.py
+++ b/solution.py
@@ -21,7 +21,12 @@
     row_share = weight_local.shape[0]
     columns = weight_local.shape[1]
     inverse = 1.0 / token_count
-    owned = lax.all_to_all(inputs_local, "fsdp", split_axis=1, concat_axis=0, tiled=True)
+    owned = jnp.concatenate(
+        lax.all_to_all(
+            jnp.stack(jnp.split(inputs_local, lax.axis_size("fsdp"), axis=1)), "fsdp", 0, 0
+        ),
+        axis=0,
+    )
     cot_all, micro_all = (
         lax.all_gather(incoming, "fsdp", axis=0, tiled=True),
         lax.all_gather(micro_ids, "fsdp", axis=1, tiled=True),

time: 95.2 us -> 83.5 us (0.88)
  blocking collectives: 52.2 us -> 38.3 us
  other arithmetic: 0 us -> 7.04 us
  local copies, waits for them, and re-layouts: 8.82 us -> 6.28 us
  matrix products: 17.4 us -> 15.5 us
    all_gather x1, blocking collectives: 32 us -> 15.9 us  [body(): lax.all_gather(incoming, 'fsdp', axis=0, tiled=True)]
    convert_element_type x0 -> x1, other arithmetic: none -> 5.93 us  [body(): partial_value.astype(jnp.bfloat16)]
    all_to_all x2 -> x0, local copies, waits for them, and re-layouts: 2.61 us -> none  [body(): lax.all_to_all(inputs_local, 'fsdp', split_axis=1, concat_axis=0, tiled=T...]
    unnamed x12 -> x9, local copies, waits for them, and re-layouts: 3.8 us -> 1.28 us
    ppermute x1, waiting for transfers between devices: 2.52 us -> 0.01 us  [from_behind(): return lax.ppermute(value, axis, pairs)]
    all_to_all x1, waiting for transfers between devices: 0.01 us -> 2.48 us  [body(): lax.all_to_all(owner_cols, 'fsdp', split_axis=0, concat_axis=1, tiled=True)]
    unnamed x1, blocking collectives: 20.2 us -> 22.4 us
    another operation x0 -> x1, local copies, waits for them, and re-layouts: none -> 1.38 us  [body(): jnp.stack(jnp.split(inputs_local, lax.axis_size('fsdp'), axis=1))]
  transfers between devices with their start and end apart: 3 -> 3, of which waited for: 1 -> 1; matrix products, arithmetic and copies ran while one was open for 21% -> 27% of each run, Pallas kernels for 0% -> 0%
where the time goes in v1:
time: 83.5 us; the launch traced here: 83.1 us
  blocking collectives  38.3 us (46%)
  matrix products  15.5 us (19%)
  starting transfers between devices  12.2 us (15%)
  other arithmetic  7.04 us (8%)
  local copies, waits for them, and re-layouts  6.28 us (8%)
  waiting for transfers between devices  2.49 us (3%)
  between operations  1.36 us (2%)
    unnamed x1, blocking collectives  22.4 us
    all_gather x1, blocking collectives, body(): lax.all_gather(incoming, 'fsdp', axis=0, tiled=True)  15.9 us
    dot_general x1, matrix products, body(): stacked = jnp.einsum('fm,fdc->mdc', onehot, partial_value)  12.5 us
    all_to_all x1, starting transfers between devices, body(): lax.all_to_all(jnp.stack(jnp.split(inputs_local, lax.axis_size('fsdp'), a...  6.35 us
    convert_element_type x1, other arithmetic, body(): partial_value.astype(jnp.bfloat16)  5.93 us
    all_to_all x1, starting transfers between devices, body(): lax.all_to_all(owner_cols, 'fsdp', split_axis=0, concat_axis=1, tiled=True)  4.23 us
    all_to_all x1, waiting for transfers between devices, body(): lax.all_to_all(owner_cols, 'fsdp', split_axis=0, concat_axis=1, tiled=True)  2.48 us
    all_to_all x1, local copies, waits for them, and re-layouts, body(): lax.all_to_all(owner_cols, 'fsdp', split_axis=0, concat_axis=1, tiled=True)  2.04 us
  transfers between devices with their start and end apart: 3, of which 1 were waited for; matrix products, arithmetic and copies ran while one was open for 27% of the time, Pallas kernels for 0%

profile of v1, /device:TPU:0, one launch (start us, length us, event | category | flops | bytes accessed | tf_op | source)
XLA Modules:
  0.0 83.1 jit_solution(13408158782730606754)
XLA Ops:
  0.6 0.0 copy-start
  0.6 0.0 copy-start.2
  0.7 0.0 copy-start.1
  0.7 1.4 %slice_bitcast_fusion.3 = (bf16[1,128,1024]{2,1,0:T(8,128)(2,1)S(1)}, bf16[1,128,1024]{2,1,0:T(8,128)(2,1)S(1)}, bf16[1,128,1024]{2,1,0:T(8,128)(2,1)S(1)}, bf16[1,128,1024]{2,1,0:T(8,128)(2,1)S(1)}) fusion(bf16[128,4096]{1,0:T(8,128)(2,1)} %bitcast.32), kind=kLoop, calls=%fused_computation.10 | loop fusion | bytes 2097152 | tf_op jit(solution)/shard_map/stack | solution.py:26
  2.0 1.1 %pad_maximum_fusion = bf16[4,128,1024]{2,1,0:T(8,128)(2,1)} fusion(bf16[1,128,1024]{2,1,0:T(8,128)(2,1)S(1)} %get-tuple-element.6, bf16[1,128,1024]{2,1,0:T(8,128)(2,1)S(1)} %get-tuple-element.7, bf16[1,128,1024]{2,1,0:T(8,128)(2,1)S(1)} %get-tuple-element.8, bf16[1,128,1024]{2,1,0:T(8,128)(2,1)S(1)} %get-tuple-element.5), kind=kLoop, calls=%fused_computation.4 | loop fusion | flops 1572864 | bytes 2097152 | tf_op jit(solution)/shard_map/stack | solution.py:26
  3.2 6.3 %all-to-all-start.1 = ((bf16[4,128,1024]{2,1,0:T(8,128)(2,1)}), bf16[4,128,1024]{2,1,0:T(8,128)(2,1)S(1)}, u32[]{:S(2)}, u32[]{:S(2)}) async-start(bf16[4,128,1024]{2,1,0:T(8,128)(2,1)} %pad_maximum_fusion), calls=%async_computation.1 | async-start | bytes 2097152 | tf_op jit(solution)/shard_map/all_to_all | solution.py:25
  9.5 0.0 copy-done.1
  9.5 1.6 %collective-permute-start = (bf16[1,128,512]{2,1,0:T(8,128)(2,1)S(1)}, bf16[1,128,512]{2,1,0:T(8,128)(2,1)S(1)}, u32[]{:S(2)}, u32[]{:S(2)}) collective-permute-start(bf16[1,128,512]{2,1,0:T(8,128)(2,1)S(1)} %copy-done.1), channel_id=1, source_target_pairs={{0,28},{4,0},{8,4},{12,8},{16,12},{20,16},{24,20},{28,24},{1,29},{... | collective-permute-start | bytes 393224 | tf_op jit(solution)/shard_map/ppermute | solution.py:12
  11.8 0.0 copy-done.2
  11.8 0.6 dynamic-slice
  12.4 0.7 bitcast_dynamic-update-slice_fusion
  13.0 22.4 %all-reduce = s32[4]{0:T(128)S(1)} all-reduce(s32[4]{0:T(128)S(1)} %bitcast_dynamic-update-slice_fusion), channel_id=1, replica_groups=mesh['section'=8,'fsdp'=4] {'fsdp'}, use_global_device_ids=true, to_apply=%add | all-reduce | flops 4 | bytes 32
  35.4 0.0 collective-permute-done
  35.4 15.9 %all-gather = bf16[1,512,512]{2,1,0:T(8,128)(2,1)S(1)} all-gather(bf16[1,128,512]{2,1,0:T(8,128)(2,1)S(1)} %collective-permute-done), channel_id=2, replica_groups=mesh['section'=8,'fsdp'=4] {'fsdp'}, dimensions={1}, use_global_device_ids=true | all-gather | bytes 655360 | tf_op jit(solution)/shard_map/all_gather | solution.py:31
  51.3 0.0 copy-done
  51.3 1.7 %convolution_convert_fusion = bf16[512,1024]{1,0:T(8,128)(2,1)} fusion(bf16[1,1024,512]{2,1,0:T(8,128)(2,1)S(1)} %copy-done, bf16[1,512,512]{2,1,0:T(8,128)(2,1)S(1)} %all-gather), kind=kOutput, calls=%fused_computation.3 | convolution fusion | flops 537395200 | bytes 2621440 | tf_op jit(solution)/shard_map/dot_general | solution.py:34
  53.0 0.0 all-to-all-done.1
  53.0 4.2 %all-to-all-start = ((bf16[4,128,1024]{2,1,0:T(8,128)(2,1)}), bf16[4,128,1024]{2,1,0:T(8,128)(2,1)}, u32[]{:S(2)}, u32[]{:S(2)}) async-start(bf16[4,128,1024]{2,1,0:T(8,128)(2,1)} %bitcast.33), calls=%async_computation | async-start | bytes 2097152 | tf_op jit(solution)/shard_map/all_to_all | solution.py:37
  57.3 1.3 %fusion.8 = f32[4,1024,512]{2,1,0:T(8,128)S(1)} fusion(bf16[4,128,1024]{2,1,0:T(8,128)(2,1)S(1)} %all-to-all-done.1, bf16[4,128,512]{2,1,0:T(8,128)(2,1)S(1)} %bitcast.31), kind=kOutput, calls=%fused_computation.17 | convolution fusion | flops 536870912 | bytes 9961472 | tf_op jit(solution)/shard_map/ftd,ftc->fdc/dot_general | solution.py:41
  58.6 5.9 %fusion = bf16[4,1024,512]{2,0,1:T(4,128)(2,1)S(1)} fusion(f32[4,1024,512]{2,1,0:T(8,128)S(1)} %fusion.8), kind=kLoop, calls=%fused_computation.1 | loop fusion | flops 4194304 | bytes 12582912 | tf_op jit(solution)/shard_map/convert_element_type | solution.py:43
  64.5 12.5 %multiply_reduce_fusion = (f32[1024,512]{1,0:T(8,128)}, f32[1024,512]{1,0:T(8,128)}) fusion(bf16[4,1024,512]{2,0,1:T(4,128)(2,1)S(1)} %fusion, s32[4]{0:T(128)S(1)} %all-reduce), kind=kOutput, calls=%fused_computation.2 | convolution fusion | flops 10485768 | bytes 8388624 | tf_op jit(solution)/shard_map/fm,fdc->mdc/dot_general | solution.py:47
  77.0 2.5 %all-to-all-done = bf16[4,128,1024]{2,1,0:T(8,128)(2,1)} async-done(((bf16[4,128,1024]{2,1,0:T(8,128)(2,1)}), bf16[4,128,1024]{2,1,0:T(8,128)(2,1)}, u32[]{:S(2)}, u32[]{:S(2)}) %all-to-all-start) | async-done | bytes 1048608 | tf_op jit(solution)/shard_map/all_to_all | solution.py:37
  79.5 2.0 %copy.7 = bf16[128,4,1024]{2,1,0:T(4,128)(2,1)S(1)} copy(bf16[128,4,1024]{2,0,1:T(8,128)(2,1)} %bitcast.3) | data formatting | bytes 2097152 | tf_op jit(solution)/shard_map/all_to_all | solution.py:37
  81.5 1.6 %broadcast_in_dim.10 = bf16[1,128,4096]{2,1,0:T(8,128)(2,1)} reshape(bf16[128,4,1024]{2,1,0:T(4,128)(2,1)S(1)} %copy.7) | data formatting | bytes 2097152 | tf_op jit(solution)/shard_map/broadcast_in_dim | solution.py:50
  (1 shorter events, 0.0 us)
Async XLA Ops:
  0.6 50.7 %copy-start = (bf16[1,1024,512]{2,1,0:T(8,128)(2,1)S(1)}, bf16[1,1024,512]{2,1,0:T(8,128)(2,1)}, u32[]{:S(2)}) copy-start(bf16[1,1024,512]{2,1,0:T(8,128)(2,1)} %param.6) | copy-start | bytes 3145732
  0.6 11.1 %copy-start.2 = (u32[32]{0:T(128)S(1)}, u32[32]{0:T(128)}, u32[]{:S(2)}) copy-start(u32[32]{0:T(128)} %constant.10) | copy-start | bytes 388
  0.7 8.8 %copy-start.1 = (bf16[1,128,512]{2,1,0:T(8,128)(2,1)S(1)}, bf16[1,128,512]{2,1,0:T(8,128)(2,1)}, u32[]{:S(2)}) copy-start(bf16[1,128,512]{2,1,0:T(8,128)(2,1)} %param.5) | copy-start | bytes 393220
  3.2 49.9 %all-to-all-start.1 = ((bf16[4,128,1024]{2,1,0:T(8,128)(2,1)}), bf16[4,128,1024]{2,1,0:T(8,128)(2,1)S(1)}, u32[]{:S(2)}, u32[]{:S(2)}) async-start(bf16[4,128,1024]{2,1,0:T(8,128)(2,1)} %pad_maximum_fusion), calls=%async_computation.1 | async-start | bytes 2097152 | tf_op jit(solution)/shard_map/all_to_all | solution.py:25
  9.5 25.9 %collective-permute-start = (bf16[1,128,512]{2,1,0:T(8,128)(2,1)S(1)}, bf16[1,128,512]{2,1,0:T(8,128)(2,1)S(1)}, u32[]{:S(2)}, u32[]{:S(2)}) collective-permute-start(bf16[1,128,512]{2,1,0:T(8,128)(2,1)S(1)} %copy-done.1), channel_id=1, source_target_pairs={{0,28},{4,0},{8,4},{12,8},{16,12},{20,16},{24,20},{28,24},{1,29},{... | collective-permute-start | bytes 393224 | tf_op jit(solution)/shard_map/ppermute | solution.py:12
  53.0 26.5 %all-to-all-start = ((bf16[4,128,1024]{2,1,0:T(8,128)(2,1)}), bf16[4,128,1024]{2,1,0:T(8,128)(2,1)}, u32[]{:S(2)}, u32[]{:S(2)}) async-start(bf16[4,128,1024]{2,1,0:T(8,128)(2,1)} %bitcast.33), calls=%async_computation | async-start | bytes 2097152 | tf_op jit(solution)/shard_map/all_to_all | solution.py:37
